TPU v7x, 256 devices: a whole 4x4x8 slice. The times are simulated.
256 devices in a mesh: space: 32 (over y, x, z_hi), band: 8 (over z_lo, core).
Axes of the slice: x: 4, y: 4, z: 8 (z_hi: 2, z_lo: 4; z = z_hi * 4 + z_lo), core: 2. Of those that a mesh axis runs over, the one named last changes fastest.
Arguments:
- orbitals: float32 [64, 192, 32, 128], P('band', 'space'), may hold values from -18 to 18
- previous: float32 [64, 192, 32, 128], P('band', 'space'), may hold values from -18 to 18
- potential: float32 [192, 32, 128], P('space'), may hold values from -4 to 4
- projectors: bfloat16 [128, 9, 6, 32, 128], P('space'), may hold values from -0.1875 to 0.1875
- strengths: float32 [128, 9], replicated, may hold values from -3 to 3
- atom_planes: int32 [128], replicated, may hold values from 0 to 191, as said below
Outputs:
- filtered: bfloat16 [64, 192, 32, 128], P('band', 'space')
- margin: float32 [64, 64], P('space', 'band')
- projection: float32 [64, 64], P('space', 'band')
Inputs may be any that keep to these rules, and one draw needn't show every extreme that they name: `atom_planes`: entry a is the first plane of atom a's box of 6 planes. In each aligned block of 4 entries (block s) every box starts at one of the planes s * 6 to s * 6 + 5, and in every block one atom starts at the first of these planes and another at the last.
All inputs are finite; a program needn't handle non-finite values.
Results may differ from a plain program's by a relative error of at most 0.0065.
Values may be sent and summed in bfloat16 or wider, within the bound.
A program may use at most 192 MiB of HBM per device.

v0:
```python
import jax
import jax.numpy as jnp
from jax import lax
from jax.sharding import PartitionSpec as P

HALO = 6
BOX = 6
NPJ = 9
stencil_weights = (
    -5369.0 / 1800.0,
    12.0 / 7.0,
    -15.0 / 56.0,
    10.0 / 189.0,
    -1.0 / 112.0,
    2.0 / 1925.0,
    -1.0 / 16632.0,
)
center = 5.5
halfwidth = 5.5


def with_halo(block, sides, width):
    for axis, dim in sides:
        count = lax.axis_size(axis)
        forward = [(i, i + 1) for i in range(count - 1)]
        forward.append((count - 1, 0))
        backward = [(target, source) for source, target in forward]
        low = lax.ppermute(
            lax.slice_in_dim(block, block.shape[dim] - width, None, axis=dim), axis, forward
        )
        high = lax.ppermute(lax.slice_in_dim(block, 0, width, axis=dim), axis, backward)
        block = jnp.concatenate([low, block, high], axis=dim)
    return block


def shifted(value, axis, steps):
    count = lax.axis_size(axis)
    pairs = [(source, (source + steps) % count) for source in range(count)]
    return lax.ppermute(value, axis, pairs)


def laplace_axis(field, axis):
    total = stencil_weights[0] * field
    for offset in range(1, HALO + 1):
        total = total + stencil_weights[offset] * (
            jnp.roll(field, offset, axis) + jnp.roll(field, -offset, axis)
        )
    return total


def place_table(first_planes, projector_block, base, window, total_planes):
    box_rows = jnp.arange(BOX, dtype=jnp.int32)
    planes_out = jnp.arange(window, dtype=jnp.int32)
    relative = (first_planes[:, None] + box_rows[None, :] - base) % total_planes
    placer = (planes_out[None, None, :] == relative[:, :, None]).astype(jnp.float32)
    return jnp.einsum(
        "apq,ajpyz->ajqyz",
        placer,
        projector_block.astype(jnp.float32),
        precision=lax.Precision.HIGHEST,
    )


def shards(orbitals, previous, potential, projectors, strengths, atom_planes):
    band_dev, slab_planes, cells_y, cells_z = orbitals.shape
    space_count = lax.axis_size("space")
    total_planes = slab_planes * space_count
    extended = with_halo(orbitals, (("space", 1),), HALO)
    along_x = stencil_weights[0] * orbitals
    for offset in range(1, HALO + 1):
        ahead = extended[:, HALO + offset : HALO + offset + slab_planes]
        behind = extended[:, HALO - offset : HALO - offset + slab_planes]
        along_x = along_x + stencil_weights[offset] * (ahead + behind)
    kinetic = -0.5 * (along_x + laplace_axis(orbitals, 2) + laplace_axis(orbitals, 3))
    device_index = lax.axis_index("space")
    atom_count = projectors.shape[0]
    own_start = device_index * atom_count
    own_planes = lax.dynamic_slice_in_dim(atom_planes, own_start, atom_count, 0)
    own_strengths = lax.dynamic_slice_in_dim(strengths, own_start, atom_count, 0)
    table = place_table(
        own_planes, projectors, device_index * slab_planes, slab_planes + HALO, total_planes
    )
    table_flat = table.reshape(atom_count * NPJ, -1)
    upper = extended[:, HALO:].reshape(band_dev, -1)
    coefficients = lax.dot_general(
        table_flat,
        upper,
        (((1,), (1,)), ((), ())),
        precision=lax.Precision.HIGHEST,
        preferred_element_type=jnp.float32,
    )
    weighted = coefficients * own_strengths.reshape(-1)[:, None]
    added = lax.dot_general(
        weighted,
        table_flat,
        (((0,), (0,)), ((), ())),
        precision=lax.Precision.HIGHEST,
        preferred_element_type=jnp.float32,
    )
    added = added.reshape(band_dev, slab_planes + HALO, cells_y, cells_z)
    arrived = shifted(added[:, slab_planes:].astype(jnp.bfloat16), "space", 1).astype(jnp.float32)
    padding = jnp.zeros((band_dev, slab_planes - HALO, cells_y, cells_z), jnp.float32)
    projected_term = added[:, :slab_planes] + jnp.concatenate([arrived, padding], 1)
    hamil = kinetic + potential[None] * orbitals + projected_term
    filtered = (2.0 / halfwidth * (hamil - center * orbitals) - previous).astype(jnp.bfloat16)
    scale = 1.0 / (slab_planes * space_count * cells_y * cells_z)
    filtered_flat = filtered.reshape(band_dev, -1)
    panel_flat = orbitals.astype(jnp.bfloat16).reshape(band_dev, -1)
    columns_right = jnp.concatenate([filtered_flat, panel_flat], 0)
    piece = lax.all_gather(filtered, "band", axis=0, tiled=True)
    rows = piece.reshape(piece.shape[0], -1)
    products = lax.dot_general(
        rows, columns_right, (((1,), (1,)), ((), ())), preferred_element_type=jnp.float32
    )
    partial_sums = products * scale
    shares = lax.psum_scatter(partial_sums, "space", scatter_dimension=0, tiled=True)
    margin = shares[:, :band_dev]
    projection = shares[:, band_dev:]
    return (filtered, margin, projection)


def solution(mesh):
    in_specs = (
        P("band", "space", None, None),
        P("band", "space", None, None),
        P("space", None, None),
        P("space", None, None, None, None),
        P(),
        P(),
    )
    out_specs = (P("band", "space", None, None), P("space", "band"), P("space", "band"))
    return jax.shard_map(shards, mesh=mesh, in_specs=in_specs, out_specs=out_specs, check_vma=False)
```

profile of v0, /device:TPU:32, one launch (start us, length us, event | category | flops | bytes accessed | tf_op | source)
XLA Modules:
  0.0 414.5 jit_solution(45234726132586732)
XLA Ops:
  7.2 1.7 copy.130
  8.9 6.4 %collective-permute-start.1 = (f32[8,6,32,128]{3,0,2,1:T(8,128)S(1)}, f32[8,6,32,128]{3,0,2,1:T(8,128)S(1)}, u32[]{:S(2)}, u32[]{:S(2)}) collective-permute-start(f32[8,6,32,128]{3,0,2,1:T(8,128)S(1)} %copy.130), channel_id=1, source_target_pairs={{0,8},{8,16},{16,24},{24,32},{32,40},{40,48},{48,56},{56,64},{64,7... | collective-permute-start | bytes 2359304 | tf_op jit(solution)/shard_map/ppermute | solution.py:28
  15.3 4.7 %collective-permute-start = (f32[8,6,32,128]{3,0,2,1:T(8,128)S(1)}, f32[8,6,32,128]{3,0,2,1:T(8,128)}, u32[]{:S(2)}, u32[]{:S(2)}) collective-permute-start(f32[8,6,32,128]{3,0,2,1:T(8,128)S(1)} %copy.130), channel_id=1, source_target_pairs={{8,0},{16,8},{24,16},{32,24},{40,32},{48,40},{56,48},{64,56},{72,6... | collective-permute-start | bytes 2359304 | tf_op jit(solution)/shard_map/ppermute | solution.py:31
  20.0 1.2 fusion.86
  21.3 1.2 fusion.84
  22.5 1.2 fusion.82
  23.7 0.7 fusion.83
  24.3 1.2 fusion.80
  25.5 0.7 fusion.81
  26.2 1.2 fusion.78
  27.4 0.7 fusion.79
  28.1 1.1 fusion.76
  29.2 0.7 fusion.77
  29.9 1.4 fusion.74
  31.3 1.4 fusion.75
  32.8 1.5 fusion.72
  34.2 1.4 fusion.73
  35.7 1.4 fusion.70
  37.1 1.4 fusion.71
  38.5 1.4 fusion.68
  39.9 1.4 fusion.69
  41.3 1.5 fusion.66
  43.0 1.7 convolution_bitcast_fusion
  44.7 5.9 %copy.185 = f32[4,9,12,32,128]{4,3,2,1,0:T(8,128)} copy(f32[4,9,12,32,128]{4,2,3,1,0:T(8,128)S(1)} %convolution_bitcast_fusion) | data formatting | bytes 14155776 | tf_op jit(solution)/shard_map/apq,ajpyz->ajqyz/transpose | solution.py:56
  50.7 7.8 %reshape.53 = f32[36,49152]{1,0:T(8,128)} reshape(f32[4,9,12,32,128]{4,3,2,1,0:T(8,128)} %copy.185) | data formatting | bytes 14155776 | tf_op jit(solution)/shard_map/reshape | solution.py:83
  58.4 1.5 fusion.67
  60.2 4.7 %copy.194 = f32[5,8,384,128]{3,2,1,0:T(8,128)S(1)} copy(f32[5,8,384,128]{3,1,2,0:T(8,128)} %bitcast.38) | data formatting | bytes 15728640
  64.8 0.7 slice.369
  65.6 1.4 fusion.64
  67.0 1.6 collective-permute-done.1
  68.7 0.5 constant_dynamic-update-slice_fusion.2
  69.1 3.2 collective-permute-done
  72.3 1.2 constant_dynamic-update-slice_fusion
  73.5 6.2 %fusion.9 = f32[36,8,1,1]{0,1,3,2:T(8,128)S(1)} fusion(f32[36,49152]{1,0:T(8,128)S(1)} %bitcast.40, f32[8,49152]{1,0:T(8,128)S(1)} %bitcast.43, f32[36]{0:T(128)S(1)} %mul.132), kind=kOutput, calls=%fused_computation.9 | convolution fusion | flops 169869600 | bytes 8652048 | tf_op jit(solution)/shard_map/dot_general | solution.py:85
  79.8 8.1 %fusion = f32[8,12,32,128]{3,0,2,1:T(8,128)S(1)} fusion(f32[36,8,1,1]{0,1,3,2:T(8,128)S(1)} %fusion.9, f32[12,32,128,36]{2,1,0,3:T(8,128)S(1)} %bitcast.41), kind=kOutput, calls=%fused_computation | convolution fusion | flops 169869312 | bytes 8651904 | tf_op jit(solution)/shard_map/dot_general | solution.py:93
  87.9 6.3 %collective-permute-start.2 = (bf16[8,6,32,128]{3,0,2,1:T(8,128)(2,1)S(1)}, bf16[8,6,32,128]{3,0,2,1:T(8,128)(2,1)}, u32[]{:S(2)}, u32[]{:S(2)}) collective-permute-start(bf16[8,6,32,128]{3,0,2,1:T(8,128)(2,1)S(1)} %slice.432), channel_id=1, source_target_pairs={{0,8},{8,16},{16,24},{24,32},{32,40},{40,48},{48,56},{56,64},{64,7... | collective-permute-start | bytes 1179656 | tf_op jit(solution)/shard_map/ppermute | solution.py:39
  94.2 1.5 fusion.65
  95.7 16.5 %collective-permute-done.2 = bf16[8,6,32,128]{3,0,2,1:T(8,128)(2,1)} collective-permute-done((bf16[8,6,32,128]{3,0,2,1:T(8,128)(2,1)S(1)}, bf16[8,6,32,128]{3,0,2,1:T(8,128)(2,1)}, u32[]{:S(2)}, u32[]{:S(2)}) %collective-permute-start.2) | collective-permute-done | bytes 393248 | tf_op jit(solution)/shard_map/ppermute | solution.py:39
  112.3 12.4 %fusion.14 = bf16[8,6,32,128]{3,0,2,1:T(8,128)(2,1)} fusion(f32[8,12,32,128]{3,0,2,1:T(8,128)S(1)} %fusion, f32[8,12,32,128]{3,0,2,1:T(8,128)S(1)} %get-tuple-element.60, f32[8,12,32,128]{3,0,2,1:T(8,128)S(1)} %constant_dynamic-update-slice_fusion, f32[8,6,31,128]{3,0,2,1:T(8,128)} %get-tuple-element.57, f32[8,6,1,128]{3,0,2,1:T(8,128)S(1)} %get-tuple-element.59, ...), kind=kLoop, calls=%fused_computation.16 | loop fusion | flops 18087936 | bytes 31555584 | tf_op jit(solution)/shard_map/convert_element_type | solution.py:105
  124.8 0.3 copy.212
  125.0 0.3 copy-done.12
  125.3 0.6 dynamic-slice
  126.6 0.8 copy.191
  127.4 50.6 %all-gather.2.cloned.1.call-done = bf16[64,6,32,128]{3,0,2,1:T(8,128)(2,1)} async-done(((bf16[8,6,32,128]{3,0,2,1:T(8,128)(2,1)}), bf16[64,6,32,128]{3,0,2,1:T(8,128)(2,1)}) %all-gather.2.cloned.1.call-update) | async-done | bytes 3145744 | tf_op jit(solution)/shard_map/all_gather | solution.py:110
  178.0 3.9 copy.190
  181.9 1.8 fusion.6
  183.8 223.2 %all-reduce = f32[64,16]{1,0:T(8,128)S(1)} all-reduce(f32[64,16]{1,0:T(8,128)S(1)} %fusion.6), channel_id=2, replica_groups=mesh['space'=32,'band'=8] {'space'}, use_global_device_ids=true, to_apply=%region_0.1.clone | all-reduce | flops 1024 | bytes 8192
  407.0 0.6 fusion.88
  (43 shorter events, 0.7 us)
Async XLA Ops:
  7.2 35.8 %copy-start = (bf16[4,9,6,32,128]{4,3,2,1,0:T(8,128)(2,1)S(1)}, bf16[4,9,6,32,128]{4,3,2,1,0:T(8,128)(2,1)}, u32[]{:S(2)}) copy-start(bf16[4,9,6,32,128]{4,3,2,1,0:T(8,128)(2,1)} %param.9) | copy-start | bytes 5308420
  7.2 170.8 %all-gather.2.cloned.1.call-start = ((), (), s32[]{:S(2)}) async-start(), calls=%async_computation | async-start | bytes 3538944 | tf_op jit(solution)/shard_map/all_gather | solution.py:110
  8.9 59.7 %collective-permute-start.1 = (f32[8,6,32,128]{3,0,2,1:T(8,128)S(1)}, f32[8,6,32,128]{3,0,2,1:T(8,128)S(1)}, u32[]{:S(2)}, u32[]{:S(2)}) collective-permute-start(f32[8,6,32,128]{3,0,2,1:T(8,128)S(1)} %copy.130), channel_id=1, source_target_pairs={{0,8},{8,16},{16,24},{24,32},{32,40},{40,48},{48,56},{56,64},{64,7... | collective-permute-start | bytes 2359304 | tf_op jit(solution)/shard_map/ppermute | solution.py:28
  15.3 57.0 %collective-permute-start = (f32[8,6,32,128]{3,0,2,1:T(8,128)S(1)}, f32[8,6,32,128]{3,0,2,1:T(8,128)}, u32[]{:S(2)}, u32[]{:S(2)}) collective-permute-start(f32[8,6,32,128]{3,0,2,1:T(8,128)S(1)} %copy.130), channel_id=1, source_target_pairs={{8,0},{16,8},{24,16},{32,24},{40,32},{48,40},{56,48},{64,56},{72,6... | collective-permute-start | bytes 2359304 | tf_op jit(solution)/shard_map/ppermute | solution.py:31
  41.3 1.5 copy-start.11
  58.4 1.5 copy-start.10
  64.8 8.7 %slice-start = ((s8[7864320]{0:T(1024)(128)(4,1)}), s8[4194304]{0:T(1024)(128)(4,1)S(1)}, s32[]{:S(2)}) async-start(s8[7864320]{0:T(1024)(128)(4,1)} %bitcast.39), calls=%async_computation.1 | async-start | bytes 8388608
  64.8 8.7 %slice-start.1 = ((s8[7864320]{0:T(1024)(128)(4,1)}), s8[3670016]{0:T(1024)(128)(4,1)S(1)}, s32[]{:S(2)}) async-start(s8[7864320]{0:T(1024)(128)(4,1)} %bitcast.39), calls=%async_computation.2 | async-start | bytes 7340032
  65.6 3.1 copy-start.2
  87.8 24.4 %copy-start.8 = (f32[8,6,32,126]{3,0,2,1:T(8,128)S(1)}, f32[8,6,32,126]{3,0,2,1:T(8,128)}, u32[]{:S(2)}) copy-start(f32[8,6,32,126]{3,0,2,1:T(8,128)} %get-tuple-element.28) | copy-start | bytes 2322436
  87.9 24.3 %copy-start.4 = (f32[8,6,32,127]{3,0,2,1:T(8,128)S(1)}, f32[8,6,32,127]{3,0,2,1:T(8,128)}, u32[]{:S(2)}) copy-start(f32[8,6,32,127]{3,0,2,1:T(8,128)} %get-tuple-element.32) | copy-start | bytes 2340868
  87.9 24.3 %copy-start.5 = (f32[8,6,32,127]{3,0,2,1:T(8,128)S(1)}, f32[8,6,32,127]{3,0,2,1:T(8,128)}, u32[]{:S(2)}) copy-start(f32[8,6,32,127]{3,0,2,1:T(8,128)} %get-tuple-element.33) | copy-start | bytes 2340868
  87.9 24.3 %copy-start.6 = (f32[8,6,32,1]{3,0,2,1:T(8,128)S(1)}, f32[8,6,32,1]{3,0,2,1:T(8,128)}, u32[]{:S(2)}) copy-start(f32[8,6,32,1]{3,0,2,1:T(8,128)} %get-tuple-element.34) | copy-start | bytes 18436
  87.9 24.3 %copy-start.7 = (f32[8,6,32,1]{3,0,2,1:T(8,128)S(1)}, f32[8,6,32,1]{3,0,2,1:T(8,128)}, u32[]{:S(2)}) copy-start(f32[8,6,32,1]{3,0,2,1:T(8,128)} %get-tuple-element.35) | copy-start | bytes 18436
  87.9 24.3 %copy-start.9 = (f32[8,6,6,128]{3,0,2,1:T(8,128)S(1)}, f32[8,6,6,128]{3,0,2,1:T(8,128)}, u32[]{:S(2)}) copy-start(f32[8,6,6,128]{3,0,2,1:T(8,128)} %get-tuple-element.39) | copy-start | bytes 442372
  87.9 24.3 %collective-permute-start.2 = (bf16[8,6,32,128]{3,0,2,1:T(8,128)(2,1)S(1)}, bf16[8,6,32,128]{3,0,2,1:T(8,128)(2,1)}, u32[]{:S(2)}, u32[]{:S(2)}) collective-permute-start(bf16[8,6,32,128]{3,0,2,1:T(8,128)(2,1)S(1)} %slice.432), channel_id=1, source_target_pairs={{0,8},{8,16},{16,24},{24,32},{32,40},{40,48},{48,56},{56,64},{64,7... | collective-permute-start | bytes 1179656 | tf_op jit(solution)/shard_map/ppermute | solution.py:39
  124.6 0.7 copy-start.12
  124.6 1.9 copy-start.3
  181.9 225.7 %copy-start.1 = (bf16[4,9,6,32,128]{4,3,2,1,0:T(8,128)(2,1)S(1)}, bf16[4,9,6,32,128]{4,3,2,1,0:T(8,128)(2,1)}, u32[]{:S(2)}) copy-start(bf16[4,9,6,32,128]{4,3,2,1,0:T(8,128)(2,1)} %param.9) | copy-start | bytes 5308420
Sparse Core Ops, SparseCore 0:
  124.8 53.1 all-gather.1
where the time goes:
time: 415 us; the launch traced here: 414 us
  blocking collectives  223 us (54%)
  waiting for transfers between devices  72 us (17%)
  local copies, waits for them, and re-layouts  56.6 us (14%)
  matrix products  17.9 us (4%)
  starting transfers between devices  17.4 us (4%)
  between operations  15 us (4%)
  other arithmetic  12.5 us (3%)
    unnamed x1, blocking collectives  223 us
    all_gather x1, waiting for transfers between devices, shards(): piece = lax.all_gather(filtered, 'band', axis=0, tiled=True)  50.6 us
    slice x24, local copies, waits for them, and re-layouts, laplace_axis(): jnp.roll(field, -offset, axis)  27.1 us
    ppermute x1, waiting for transfers between devices, shifted(): return lax.ppermute(value, axis, pairs)  16.5 us
    convert_element_type x1, other arithmetic, shards(): (2.0 / halfwidth * (hamil - center * orbitals) - previous).astype(jnp.bfl...  12.4 us
    unnamed x38, local copies, waits for them, and re-layouts  9.18 us
  transfers between devices with their start and end apart: 4, of which 4 were waited for; matrix products, arithmetic and copies ran while one was open for 12% of the time, Pallas kernels for 0%

commit v1 on v0

--- a/solution.py
+++ b/solution.py
@@ -107,7 +107,9 @@
     filtered_flat = filtered.reshape(band_dev, -1)
     panel_flat = orbitals.astype(jnp.bfloat16).reshape(band_dev, -1)
     columns_right = jnp.concatenate([filtered_flat, panel_flat], 0)
-    piece = lax.all_gather(filtered, "band", axis=0, tiled=True)
+    piece = jnp.concatenate(
+        lax.all_to_all(jnp.stack([filtered] * lax.axis_size("band")), "band", 0, 0), axis=0
+    )
     rows = piece.reshape(piece.shape[0], -1)
     products = lax.dot_general(
         rows, columns_right, (((1,), (1,)), ((), ())), preferred_element_type=jnp.float32

time: 415 us -> 437 us (1.053)
  starting transfers between devices: 17.4 us -> 33.9 us
  waiting for transfers between devices: 72 us -> 87.4 us
  between operations: 15 us -> 1.55 us
    all_to_all x0 -> x1, waiting for transfers between devices: none -> 66.2 us  [shards(): lax.all_to_all(jnp.stack([filtered] * lax.axis_size('band')), 'band', 0, 0)]
    all_gather x1 -> x0, waiting for transfers between devices: 50.6 us -> none  [shards(): piece = lax.all_gather(filtered, 'band', axis=0, tiled=True)]
    all_to_all x0 -> x1, starting transfers between devices: none -> 16.5 us  [shards(): lax.all_to_all(jnp.stack([filtered] * lax.axis_size('band')), 'band', 0, 0)]
    another operation x0 -> x2, local copies, waits for them, and re-layouts: none -> 7.2 us  [the longest x1 4.75 us: shards(): rows = piece.reshape(piece.shape[0], -1)]
    unnamed x38 -> x40, local copies, waits for them, and re-layouts: 9.18 us -> 9.22 us
  transfers between devices with their start and end apart: 4 -> 4, of which waited for: 4 -> 4; matrix products, arithmetic and copies ran while one was open for 12% -> 11% of each run, Pallas kernels for 0% -> 0%
where the time goes in v1:
time: 437 us; the launch traced here: 434 us
  blocking collectives  221 us (51%)
  waiting for transfers between devices  87.4 us (20%)
  local copies, waits for them, and re-layouts  59.9 us (14%)
  starting transfers between devices  33.9 us (8%)
  matrix products  19 us (4%)
  other arithmetic  12 us (3%)
    unnamed x1, blocking collectives  221 us
    all_to_all x1, waiting for transfers between devices, shards(): lax.all_to_all(jnp.stack([filtered] * lax.axis_size('band')), 'band', 0, 0)  66.2 us
    slice x24, local copies, waits for them, and re-layouts, laplace_axis(): jnp.roll(field, -offset, axis)  27.1 us
    all_to_all x1, starting transfers between devices, shards(): lax.all_to_all(jnp.stack([filtered] * lax.axis_size('band')), 'band', 0, 0)  16.5 us
    ppermute x1, waiting for transfers between devices, shifted(): return lax.ppermute(value, axis, pairs)  16.4 us
    convert_element_type x1, other arithmetic, shards(): (2.0 / halfwidth * (hamil - center * orbitals) - previous).astype(jnp.bfl...  11.9 us
    unnamed x40, local copies, waits for them, and re-layouts  9.22 us
  transfers between devices with their start and end apart: 4, of which 4 were waited for; matrix products, arithmetic and copies ran while one was open for 11% of the time, Pallas kernels for 0%

profile of v1, /device:TPU:32, one launch (start us, length us, event | category | flops | bytes accessed | tf_op | source)
XLA Modules:
  0.0 434.2 jit_solution(15196816345287288907)
XLA Ops:
  0.6 1.7 copy.131
  2.4 6.4 %collective-permute-start.1 = (f32[8,6,32,128]{3,0,2,1:T(8,128)S(1)}, f32[8,6,32,128]{3,0,2,1:T(8,128)S(1)}, u32[]{:S(2)}, u32[]{:S(2)}) collective-permute-start(f32[8,6,32,128]{3,0,2,1:T(8,128)S(1)} %copy.131), channel_id=1, source_target_pairs={{0,8},{8,16},{16,24},{24,32},{32,40},{40,48},{48,56},{56,64},{64,7... | collective-permute-start | bytes 2359304 | tf_op jit(solution)/shard_map/ppermute | solution.py:28
  8.7 4.7 %collective-permute-start = (f32[8,6,32,128]{3,0,2,1:T(8,128)S(1)}, f32[8,6,32,128]{3,0,2,1:T(8,128)}, u32[]{:S(2)}, u32[]{:S(2)}) collective-permute-start(f32[8,6,32,128]{3,0,2,1:T(8,128)S(1)} %copy.131), channel_id=1, source_target_pairs={{8,0},{16,8},{24,16},{32,24},{40,32},{48,40},{56,48},{64,56},{72,6... | collective-permute-start | bytes 2359304 | tf_op jit(solution)/shard_map/ppermute | solution.py:31
  13.5 1.2 fusion.80
  14.7 1.2 fusion.78
  15.9 1.2 fusion.76
  17.1 0.7 fusion.77
  17.7 1.2 fusion.74
  19.0 0.7 fusion.75
  19.7 1.2 fusion.72
  20.8 0.7 fusion.73
  21.6 1.1 fusion.70
  22.7 0.7 fusion.71
  23.4 1.4 fusion.68
  24.8 1.4 fusion.69
  26.2 1.5 fusion.66
  27.7 1.4 fusion.67
  29.1 1.4 fusion.64
  30.5 1.4 fusion.65
  31.9 1.4 fusion.62
  33.4 1.4 fusion.63
  34.8 1.5 fusion.60
  36.4 1.7 convolution_bitcast_fusion
  38.2 5.9 %copy.186 = f32[4,9,12,32,128]{4,3,2,1,0:T(8,128)} copy(f32[4,9,12,32,128]{4,2,3,1,0:T(8,128)S(1)} %convolution_bitcast_fusion) | data formatting | bytes 14155776 | tf_op jit(solution)/shard_map/apq,ajpyz->ajqyz/transpose | solution.py:56
  44.1 7.8 %reshape.52 = f32[36,49152]{1,0:T(8,128)} reshape(f32[4,9,12,32,128]{4,3,2,1,0:T(8,128)} %copy.186) | data formatting | bytes 14155776 | tf_op jit(solution)/shard_map/reshape | solution.py:83
  51.9 1.5 fusion.61
  53.6 4.7 %copy.195 = f32[5,8,384,128]{3,2,1,0:T(8,128)S(1)} copy(f32[5,8,384,128]{3,1,2,0:T(8,128)} %bitcast.34) | data formatting | bytes 15728640
  58.3 0.7 slice.369
  59.0 1.4 fusion.58
  60.4 1.6 collective-permute-done.1
  62.1 0.5 constant_dynamic-update-slice_fusion.2
  62.6 3.2 collective-permute-done
  65.8 1.2 constant_dynamic-update-slice_fusion
  67.0 6.2 %fusion.3 = f32[36,8,1,1]{0,1,3,2:T(8,128)S(1)} fusion(f32[36,49152]{1,0:T(8,128)S(1)} %bitcast.36, f32[8,49152]{1,0:T(8,128)S(1)} %bitcast.39, f32[36]{0:T(128)S(1)} %mul.132), kind=kOutput, calls=%fused_computation.6 | convolution fusion | flops 169869600 | bytes 8652048 | tf_op jit(solution)/shard_map/dot_general | solution.py:85
  73.2 8.1 %fusion = f32[8,12,32,128]{3,0,2,1:T(8,128)S(1)} fusion(f32[36,8,1,1]{0,1,3,2:T(8,128)S(1)} %fusion.3, f32[12,32,128,36]{2,1,0,3:T(8,128)S(1)} %bitcast.37), kind=kOutput, calls=%fused_computation | convolution fusion | flops 169869312 | bytes 8651904 | tf_op jit(solution)/shard_map/dot_general | solution.py:93
  81.4 6.3 %collective-permute-start.2 = (bf16[8,6,32,128]{3,0,2,1:T(8,128)(2,1)S(1)}, bf16[8,6,32,128]{3,0,2,1:T(8,128)(2,1)S(1)}, u32[]{:S(2)}, u32[]{:S(2)}) collective-permute-start(bf16[8,6,32,128]{3,0,2,1:T(8,128)(2,1)S(1)} %slice.432), channel_id=1, source_target_pairs={{0,8},{8,16},{16,24},{24,32},{32,40},{40,48},{48,56},{56,64},{64,7... | collective-permute-start | bytes 1179656 | tf_op jit(solution)/shard_map/ppermute | solution.py:39
  87.7 1.5 fusion.59
  89.1 16.4 %collective-permute-done.2 = bf16[8,6,32,128]{3,0,2,1:T(8,128)(2,1)S(1)} collective-permute-done((bf16[8,6,32,128]{3,0,2,1:T(8,128)(2,1)S(1)}, bf16[8,6,32,128]{3,0,2,1:T(8,128)(2,1)S(1)}, u32[]{:S(2)}, u32[]{:S(2)}) %collective-permute-start.2) | collective-permute-done | bytes 393248 | tf_op jit(solution)/shard_map/ppermute | solution.py:39
  105.6 0.7 copy-done.10
  106.3 11.9 %fusion.8 = bf16[8,6,32,128]{3,0,2,1:T(8,128)(2,1)S(1)} fusion(f32[8,12,32,128]{3,0,2,1:T(8,128)S(1)} %fusion, f32[8,12,32,128]{3,0,2,1:T(8,128)S(1)} %get-tuple-element.60, f32[8,12,32,128]{3,0,2,1:T(8,128)S(1)} %constant_dynamic-update-slice_fusion, f32[8,6,31,128]{3,0,2,1:T(8,128)} %get-tuple-element.57, f32[8,6,1,128]{3,0,2,1:T(8,128)S(1)} %get-tuple-element.59, ...), kind=kLoop, calls=%fused_computation.13 | loop fusion | flops 18087936 | bytes 31555584 | tf_op jit(solution)/shard_map/convert_element_type | solution.py:105
  118.3 2.4 stack.2
  120.7 16.5 %all-to-all-start = ((bf16[8,8,6,32,128]{4,3,2,1,0:T(8,128)(2,1)}), bf16[8,8,6,32,128]{4,3,2,1,0:T(8,128)(2,1)}, u32[]{:S(2)}, u32[]{:S(2)}) async-start(bf16[8,8,6,32,128]{4,3,2,1,0:T(8,128)(2,1)} %stack.2), calls=%async_computation | async-start | bytes 6291456 | tf_op jit(solution)/shard_map/all_to_all | solution.py:111
  137.9 0.6 dynamic-slice
  139.2 66.2 %all-to-all-done = bf16[8,8,6,32,128]{4,3,2,1,0:T(8,128)(2,1)} async-done(((bf16[8,8,6,32,128]{4,3,2,1,0:T(8,128)(2,1)}), bf16[8,8,6,32,128]{4,3,2,1,0:T(8,128)(2,1)}, u32[]{:S(2)}, u32[]{:S(2)}) %all-to-all-start) | async-done | bytes 3145760 | tf_op jit(solution)/shard_map/all_to_all | solution.py:111
  205.3 4.7 %reshape_reshape.3 = bf16[64,24576]{1,0:T(8,128)(2,1)} reshape(bf16[8,8,6,32,128]{4,3,2,1,0:T(8,128)(2,1)} %all-to-all-done) | data formatting | bytes 6291456 | tf_op jit(solution)/shard_map/reshape;reshape | solution.py:113
  210.1 3.0 convolution_multiply_fusion
  213.1 220.5 %all-reduce = f32[64,16]{1,0:T(8,128)S(1)} all-reduce(f32[64,16]{1,0:T(8,128)S(1)} %convolution_multiply_fusion), channel_id=2, replica_groups=mesh['space'=32,'band'=8] {'space'}, use_global_device_ids=true, to_apply=%region_0.1.clone | all-reduce | flops 1024 | bytes 8192
  433.6 0.6 fusion.82
  (45 shorter events, 1.3 us)
Async XLA Ops:
  0.6 35.8 %copy-start = (bf16[4,9,6,32,128]{4,3,2,1,0:T(8,128)(2,1)S(1)}, bf16[4,9,6,32,128]{4,3,2,1,0:T(8,128)(2,1)}, u32[]{:S(2)}) copy-start(bf16[4,9,6,32,128]{4,3,2,1,0:T(8,128)(2,1)} %param.9) | copy-start | bytes 5308420
  2.4 59.7 %collective-permute-start.1 = (f32[8,6,32,128]{3,0,2,1:T(8,128)S(1)}, f32[8,6,32,128]{3,0,2,1:T(8,128)S(1)}, u32[]{:S(2)}, u32[]{:S(2)}) collective-permute-start(f32[8,6,32,128]{3,0,2,1:T(8,128)S(1)} %copy.131), channel_id=1, source_target_pairs={{0,8},{8,16},{16,24},{24,32},{32,40},{40,48},{48,56},{56,64},{64,7... | collective-permute-start | bytes 2359304 | tf_op jit(solution)/shard_map/ppermute | solution.py:28
  8.7 57.0 %collective-permute-start = (f32[8,6,32,128]{3,0,2,1:T(8,128)S(1)}, f32[8,6,32,128]{3,0,2,1:T(8,128)}, u32[]{:S(2)}, u32[]{:S(2)}) collective-permute-start(f32[8,6,32,128]{3,0,2,1:T(8,128)S(1)} %copy.131), channel_id=1, source_target_pairs={{8,0},{16,8},{24,16},{32,24},{40,32},{48,40},{56,48},{64,56},{72,6... | collective-permute-start | bytes 2359304 | tf_op jit(solution)/shard_map/ppermute | solution.py:31
  34.8 1.5 copy-start.12
  51.9 1.5 copy-start.11
  58.2 8.7 %slice-start = ((s8[7864320]{0:T(1024)(128)(4,1)}), s8[4194304]{0:T(1024)(128)(4,1)S(1)}, s32[]{:S(2)}) async-start(s8[7864320]{0:T(1024)(128)(4,1)} %bitcast.35), calls=%async_computation.1 | async-start | bytes 8388608
  58.3 8.7 %slice-start.1 = ((s8[7864320]{0:T(1024)(128)(4,1)}), s8[3670016]{0:T(1024)(128)(4,1)S(1)}, s32[]{:S(2)}) async-start(s8[7864320]{0:T(1024)(128)(4,1)} %bitcast.35), calls=%async_computation.2 | async-start | bytes 7340032
  59.0 3.1 copy-start.2
  81.3 25.0 %copy-start.7 = (f32[8,6,32,126]{3,0,2,1:T(8,128)S(1)}, f32[8,6,32,126]{3,0,2,1:T(8,128)}, u32[]{:S(2)}) copy-start(f32[8,6,32,126]{3,0,2,1:T(8,128)} %get-tuple-element.28) | copy-start | bytes 2322436
  81.3 25.0 %copy-start.3 = (f32[8,6,32,127]{3,0,2,1:T(8,128)S(1)}, f32[8,6,32,127]{3,0,2,1:T(8,128)}, u32[]{:S(2)}) copy-start(f32[8,6,32,127]{3,0,2,1:T(8,128)} %get-tuple-element.32) | copy-start | bytes 2340868
  81.3 25.0 %copy-start.4 = (f32[8,6,32,127]{3,0,2,1:T(8,128)S(1)}, f32[8,6,32,127]{3,0,2,1:T(8,128)}, u32[]{:S(2)}) copy-start(f32[8,6,32,127]{3,0,2,1:T(8,128)} %get-tuple-element.33) | copy-start | bytes 2340868
  81.3 25.0 %copy-start.5 = (f32[8,6,32,1]{3,0,2,1:T(8,128)S(1)}, f32[8,6,32,1]{3,0,2,1:T(8,128)}, u32[]{:S(2)}) copy-start(f32[8,6,32,1]{3,0,2,1:T(8,128)} %get-tuple-element.34) | copy-start | bytes 18436
  81.4 25.0 %copy-start.6 = (f32[8,6,32,1]{3,0,2,1:T(8,128)S(1)}, f32[8,6,32,1]{3,0,2,1:T(8,128)}, u32[]{:S(2)}) copy-start(f32[8,6,32,1]{3,0,2,1:T(8,128)} %get-tuple-element.35) | copy-start | bytes 18436
  81.4 25.0 %copy-start.9 = (f32[8,6,6,128]{3,0,2,1:T(8,128)S(1)}, f32[8,6,6,128]{3,0,2,1:T(8,128)}, u32[]{:S(2)}) copy-start(f32[8,6,6,128]{3,0,2,1:T(8,128)} %get-tuple-element.39) | copy-start | bytes 442372
  81.4 24.2 %collective-permute-start.2 = (bf16[8,6,32,128]{3,0,2,1:T(8,128)(2,1)S(1)}, bf16[8,6,32,128]{3,0,2,1:T(8,128)(2,1)S(1)}, u32[]{:S(2)}, u32[]{:S(2)}) collective-permute-start(bf16[8,6,32,128]{3,0,2,1:T(8,128)(2,1)S(1)} %slice.432), channel_id=1, source_target_pairs={{0,8},{8,16},{16,24},{24,32},{32,40},{40,48},{48,56},{56,64},{64,7... | collective-permute-start | bytes 1179656 | tf_op jit(solution)/shard_map/ppermute | solution.py:39
  105.6 0.7 copy-start.10
  118.3 2.5 copy-start.8
  120.7 84.6 %all-to-all-start = ((bf16[8,8,6,32,128]{4,3,2,1,0:T(8,128)(2,1)}), bf16[8,8,6,32,128]{4,3,2,1,0:T(8,128)(2,1)}, u32[]{:S(2)}, u32[]{:S(2)}) async-start(bf16[8,8,6,32,128]{4,3,2,1,0:T(8,128)(2,1)} %stack.2), calls=%async_computation | async-start | bytes 6291456 | tf_op jit(solution)/shard_map/all_to_all | solution.py:111
  137.3 0.7 copy-start.13
  210.1 224.2 %copy-start.1 = (bf16[4,9,6,32,128]{4,3,2,1,0:T(8,128)(2,1)S(1)}, bf16[4,9,6,32,128]{4,3,2,1,0:T(8,128)(2,1)}, u32[]{:S(2)}) copy-start(bf16[4,9,6,32,128]{4,3,2,1,0:T(8,128)(2,1)} %param.9) | copy-start | bytes 5308420
